TPU v7x, 256 devices: a whole 4x4x8 slice. The times are simulated.
256 devices in a mesh: space: 16 (over x_hi, z), tm: 16 (over y, x_lo, core).
Axes of the slice: x: 4 (x_hi: 2, x_lo: 2; x = x_hi * 2 + x_lo), y: 4, z: 8, core: 2. Of those that a mesh axis runs over, the one named last changes fastest.
Arguments:
- snapshots: bfloat16 [163840, 8192], P('space', 'tm'), may hold values from -6 to 6
- modes: bfloat16 [163840, 256], P('space'), may hold values from -0.015625 to 0.015625
Outputs:
- gram: float32 [4864, 4864], P('tm', 'space')
- rhs: float32 [4864, 256], P('tm', 'space')
All inputs are finite; a program needn't handle non-finite values.
Results may differ from a plain program's by a relative error of at most 0.0057.
Values may be sent and summed in bfloat16 or wider, within the bound.
A program may use at most 128 MiB of HBM per device.

v0:
```python
import jax
import jax.numpy as jnp
from jax import lax
from jax.sharding import PartitionSpec as P

LEAD_MODES = 48


ridge_weight = 0.05


def passed_along(value, axis, steps):
    count = lax.axis_size(axis)
    leading, last = (max(0, -steps), min(count, count - steps))
    return lax.ppermute(value, axis, [(source, source + steps) for source in range(leading, last)])


def build_features(current, first, second):
    steps_count = current.shape[1]
    lead = first.shape[0]
    head = current[0:lead].astype(jnp.float32)
    prod_one = (head[:, None, :] * first.astype(jnp.float32)[None, :, :]).reshape(
        lead * lead, steps_count
    )
    prod_two = (head[:, None, :] * second.astype(jnp.float32)[None, :, :]).reshape(
        lead * lead, steps_count
    )
    return jnp.concatenate([current.astype(jnp.float32), prod_one, prod_two], axis=0).astype(
        jnp.bfloat16
    )


def neighbour(values, offset):
    return passed_along(values, "tm", offset)


def contract_rows(left, right):
    return lax.dot_general(
        left, right, (((1,), (1,)), ((), ())), preferred_element_type=jnp.float32
    )


def per_device(snapshots, modes):
    partial_sums = lax.dot_general(
        modes, snapshots, (((0,), (0,)), ((), ())), preferred_element_type=jnp.float32
    )
    coeffs = lax.psum(partial_sums, "space").astype(jnp.bfloat16)
    n_space = lax.axis_size("space")
    n_time = lax.axis_size("tm")
    modes_count = coeffs.shape[0]
    snap_local = coeffs.shape[1]
    total_snaps = snap_local * n_time
    lead = LEAD_MODES
    feature_count = modes_count + 2 * lead * lead
    col_block = feature_count // n_space
    target_block = modes_count // n_space
    row_block = feature_count // n_time
    space_pos = lax.axis_index("space")
    time_pos = lax.axis_index("tm")
    moved = {}
    for offset in (1, 2, -1):
        moved[offset] = neighbour(coeffs, offset)
    phi = build_features(coeffs, moved[1][0:lead], moved[2][0:lead])
    target = moved[-1]
    right = jnp.concatenate(
        [
            lax.dynamic_slice_in_dim(phi, space_pos * col_block, col_block, 0),
            lax.dynamic_slice_in_dim(target, space_pos * target_block, target_block, 0),
        ],
        axis=0,
    )
    joined = lax.psum_scatter(contract_rows(phi, right), "tm", scatter_dimension=0, tiled=True)
    row_global = time_pos * row_block + jnp.arange(row_block, dtype=jnp.int32)
    col_global = space_pos * col_block + jnp.arange(col_block, dtype=jnp.int32)
    diagonal_mask = (row_global[:, None] == col_global[None, :]).astype(jnp.float32)
    gram = joined[:, 0:col_block] / total_snaps + ridge_weight * diagonal_mask
    rhs = joined[:, col_block:] / total_snaps
    return (gram, rhs)


def solution(mesh):
    in_specs = (P("space", "tm"), P("space", None))
    out_specs = (P("tm", "space"), P("tm", "space"))
    return jax.shard_map(
        per_device, mesh=mesh, in_specs=in_specs, out_specs=out_specs, check_vma=False
    )
```

profile of v0, /device:TPU:0, one launch (start us, length us, event | category | flops | bytes accessed | tf_op | source)
XLA Modules:
  0.0 218.7 jit_solution(5401471481429606816)
XLA Ops:
  7.2 0.0 reduce-scatter.2.cloned.1.call-start
  7.2 7.2 %fusion.6 = f32[256,512]{1,0:T(8,128)S(1)} fusion(bf16[10240,256]{1,0:T(8,128)(2,1)} %param.3, bf16[10240,512]{1,0:T(8,128)(2,1)} %param.2), kind=kOutput, calls=%fused_computation.18 | convolution fusion | flops 2684354560 | bytes 16252928 | tf_op jit(solution)/shard_map/dot_general | solution.py:44
  14.4 84.2 %all-reduce.1 = bf16[256,512]{1,0:T(8,128)(2,1)S(1)} all-reduce(f32[256,512]{1,0:T(8,128)S(1)} %fusion.6), channel_id=1, replica_groups=mesh['space'=16,'tm'=16] {'space'}, use_global_device_ids=true, to_apply=%region_0.0 | all-reduce | flops 131072 | bytes 786432 | tf_op jit(solution)/shard_map/psum | solution.py:47
  98.7 2.5 %collective-permute-start.1 = (bf16[256,512]{1,0:T(8,128)(2,1)S(1)}, bf16[256,512]{1,0:T(8,128)(2,1)S(1)}, u32[]{:S(2)}, u32[]{:S(2)}) collective-permute-start(bf16[256,512]{1,0:T(8,128)(2,1)S(1)} %all-reduce.1), channel_id=1, source_target_pairs={{0,2},{1,3},{2,4},{3,5},{4,6},{5,7},{6,8},{7,9},{8,10},{9,11},{10,... | collective-permute-start | bytes 786440 | tf_op jit(solution)/shard_map/ppermute | solution.py:15
  101.2 1.3 collective-permute-start
  102.5 1.3 collective-permute-start.2
  103.9 1.2 collective-permute-done.1
  105.1 0.0 collective-permute-done
  105.1 1.5 multiply_convert_fusion.1
  106.6 0.4 pad_maximum_fusion
  107.1 1.5 collective-permute-done.2
  108.6 8.9 %fusion.1 = f32[4864,320]{1,0:T(8,128)} fusion(bf16[16,512]{1,0:T(8,128)(2,1)S(1)} %constant_dynamic-slice_fusion, bf16[304,512]{1,0:T(8,128)(2,1)S(1)} %constant_dynamic-slice_fusion.1, bf16[2304,512]{1,0:T(8,128)(2,1)S(1)} %bitcast.7, bf16[2304,512]{1,0:T(8,128)(2,1)S(1)} %bitcast.5, bf16[256,512]{1,0:T(8,128)(2,1)S(1)} %all-reduce.1), kind=kOutput, calls=%fused_computation.5 | convolution fusion | flops 1609433088 | bytes 11534336 | tf_op jit(solution)/shard_map/dot_general | solution.py:38
  117.5 0.0 reduce-scatter.2.cloned.1.call-update
  117.6 90.7 %reduce-scatter.2.cloned.1.call-done = f32[304,320]{1,0:T(8,128)} async-done(((f32[4864,320]{1,0:T(8,128)}), f32[304,320]{1,0:T(8,128)}) %reduce-scatter.2.cloned.1.call-update) | async-done | bytes 389136 | tf_op jit(solution)/shard_map/reduce_scatter | solution.py:72
  208.2 1.0 slice_multiply_fusion.1
  209.3 0.7 copy.4
  210.0 1.9 fusion
  (6 shorter events, 0.1 us)
Async XLA Ops:
  7.2 201.1 %reduce-scatter.2.cloned.1.call-start = ((), (), s32[]{:S(2)}) async-start(), calls=%async_computation.1 | async-start | bytes 7938048 | tf_op jit(solution)/shard_map/reduce_scatter | solution.py:72
  98.7 6.4 %collective-permute-start.1 = (bf16[256,512]{1,0:T(8,128)(2,1)S(1)}, bf16[256,512]{1,0:T(8,128)(2,1)S(1)}, u32[]{:S(2)}, u32[]{:S(2)}) collective-permute-start(bf16[256,512]{1,0:T(8,128)(2,1)S(1)} %all-reduce.1), channel_id=1, source_target_pairs={{0,2},{1,3},{2,4},{3,5},{4,6},{5,7},{6,8},{7,9},{8,10},{9,11},{10,... | collective-permute-start | bytes 786440 | tf_op jit(solution)/shard_map/ppermute | solution.py:15
  101.2 3.9 %collective-permute-start = (bf16[256,512]{1,0:T(8,128)(2,1)S(1)}, bf16[256,512]{1,0:T(8,128)(2,1)S(1)}, u32[]{:S(2)}, u32[]{:S(2)}) collective-permute-start(bf16[256,512]{1,0:T(8,128)(2,1)S(1)} %all-reduce.1), channel_id=1, source_target_pairs={{0,1},{1,2},{2,3},{3,4},{4,5},{5,6},{6,7},{7,8},{8,9},{9,10},{10,1... | collective-permute-start | bytes 786440 | tf_op jit(solution)/shard_map/ppermute | solution.py:15
  102.5 6.1 %collective-permute-start.2 = (bf16[256,512]{1,0:T(8,128)(2,1)S(1)}, bf16[256,512]{1,0:T(8,128)(2,1)S(1)}, u32[]{:S(2)}, u32[]{:S(2)}) collective-permute-start(bf16[256,512]{1,0:T(8,128)(2,1)S(1)} %all-reduce.1), channel_id=1, source_target_pairs={{1,0},{2,1},{3,2},{4,3},{5,4},{6,5},{7,6},{8,7},{9,8},{10,9},{11,1... | collective-permute-start | bytes 786440 | tf_op jit(solution)/shard_map/ppermute | solution.py:15
Sparse Core Ops, SparseCore 0:
  117.7 90.5 reduce-scatter.1
where the time goes:
time: 220 us; the launch traced here: 219 us
  waiting for transfers between devices  93.4 us (42%)
  blocking collectives  84.2 us (38%)
  matrix products  16.2 us (7%)
  between operations  14.1 us (6%)
  starting transfers between devices  5.16 us (2%)
  other arithmetic  4.85 us (2%)
    reduce_scatter x1, waiting for transfers between devices, per_device(): lax.psum_scatter(contract_rows(phi, right), 'tm', scatter_dimension=0, ti...  90.7 us
    psum x1, blocking collectives, per_device(): coeffs = lax.psum(partial_sums, 'space').astype(jnp.bfloat16)  84.2 us
    dot_general x1, matrix products, contract_rows(): lax.dot_general(left, right, (((1,), (1,)), ((), ())), preferred_element_...  8.94 us
    dot_general x1, matrix products, per_device(): lax.dot_general(modes, snapshots, (((0,), (0,)), ((), ())), preferred_ele...  7.22 us
    ppermute x3, starting transfers between devices, passed_along(): lax.ppermute(value, axis, [(source, source + steps) for source in range(l...  5.13 us
  transfers between devices with their start and end apart: 4, of which 3 were waited for; matrix products, arithmetic and copies ran while one was open for 1% of the time, Pallas kernels for 0%

commit v1 on v0

v1 whole, which is shorter than its diff:
```python
import functools

import jax
import jax.numpy as jnp
from jax import lax
from jax.experimental import pallas as pl
from jax.experimental.pallas import tpu as pltpu
from jax.sharding import PartitionSpec as P

LEAD = 48
RIDGE = 0.05
GROUP = 16
MESH = pl.DeviceIdType.MESH
F32 = jnp.float32
BF16 = jnp.bfloat16


def kernel(
    n, per_block, chunks,
    snaps, modes, gram, rhs_t,
    sbuf, mbuf, psum, part, rsbuf, coef, lead, direct, head, left, right, acc, sib, fin, turned, colbuf, rowbuf,
    load_sem, rs_send, rs_recv, ag_send, ag_recv, g_send, g_recv, sib_send, sib_recv, msg_send, col_recv, row_recv,
):
    s = lax.axis_index("space")
    t = lax.axis_index("tm")
    core = lax.rem(t, 2)
    other = t + 1 - 2 * core
    rows = GROUP * per_block
    span = rows + GROUP
    dof, snap = snaps.shape
    half = snap // 2
    depth = dof // chunks
    total = n * snap
    tile0 = (rows // 128) * 128
    jblocks = LEAD // GROUP

    def loads(c):
        at = pl.ds(pl.multiple_of(c * depth, depth), depth)
        return (
            pltpu.make_async_copy(snaps.at[at, :], sbuf.at[c], load_sem.at[0, c]),
            pltpu.make_async_copy(modes.at[at, :], mbuf.at[c], load_sem.at[1, c]),
        )

    @pl.loop(0, chunks)
    def _(c):
        for copy in loads(c):
            copy.start()

    barrier = pltpu.get_barrier_semaphore()

    @pl.loop(1, n)
    def _(d):
        pl.semaphore_signal(barrier, inc=1, device_id=(lax.rem(s + d, n), t), device_id_type=MESH)
        pl.semaphore_signal(barrier, inc=1, device_id=(s, lax.rem(t + d, n)), device_id_type=MESH)

    psum[...] = jnp.zeros_like(psum)

    @pl.loop(0, chunks)
    def _(c):
        for copy in loads(c):
            copy.wait()
        psum[...] += lax.dot_general(
            mbuf[c], sbuf[c], (((0,), (0,)), ((), ())), preferred_element_type=F32
        )

    part[...] = psum[...].astype(BF16)
    pl.semaphore_wait(barrier, 2 * (n - 1))

    def group(k):
        return pl.ds(pl.multiple_of(k * GROUP, GROUP), GROUP)

    def rs_copy(d):
        peer = lax.rem(s + d, n)
        return pltpu.make_async_remote_copy(
            part.at[group(peer), :], rsbuf.at[s], rs_send.at[d], rs_recv.at[s], device_id=(peer, t), device_id_type=MESH
        )

    def rs_arrival(k):
        return pltpu.make_async_remote_copy(
            part.at[group(k), :], rsbuf.at[k], rs_send.at[0], rs_recv.at[k], device_id=(k, t), device_id_type=MESH
        )

    @pl.loop(1, n)
    def _(d):
        rs_copy(d).start()

    rsbuf[s] = part[group(s), :]

    @pl.loop(1, n)
    def _(d):
        rs_arrival(lax.rem(s + n - d, n)).wait_recv()

    value = psum[group(s), :] - rsbuf[s].astype(F32)
    for k in range(n):
        value = value + rsbuf[k].astype(F32)
    coef[group(s), :] = value.astype(BF16)

    def ag_copy(d):
        peer = lax.rem(s + d, n)
        return pltpu.make_async_remote_copy(
            coef.at[group(s), :], coef.at[group(s), :], ag_send.at[d], ag_recv.at[s], device_id=(peer, t), device_id_type=MESH
        )

    def ag_arrival(k):
        return pltpu.make_async_remote_copy(
            coef.at[group(k), :], coef.at[group(k), :], ag_send.at[0], ag_recv.at[k], device_id=(k, t), device_id_type=MESH
        )

    @pl.loop(1, n)
    def _(d):
        ag_copy(d).start()

    @pl.loop(1, n)
    def _(d):
        ag_arrival(lax.rem(s + n - d, n)).wait_recv()

    def pieces(u):
        c, pair = lax.rem(u, 2), lax.div(u, 2)
        lanes = pl.ds(pl.multiple_of(c * half, half), half)
        return (
            (coef.at[pl.ds(0, LEAD), lanes], lead.at[t + 2, pl.ds(0, LEAD), :]),
            (coef.at[group(s), lanes], lead.at[t + 2, pl.ds(LEAD, GROUP), :]),
            (coef.at[pl.ds(pl.multiple_of(pair * 2 * GROUP, 2 * GROUP), 2 * GROUP), lanes], direct.at[t]),
        )

    def g_copies(d):
        u = lax.rem(t + d, n)
        return [
            pltpu.make_async_remote_copy(src, dst, g_send.at[k, d], g_recv.at[k, t], device_id=(s, u), device_id_type=MESH)
            for k, (src, dst) in enumerate(pieces(u))
        ]

    def g_arrivals(u):
        dsts = (lead.at[u + 2, pl.ds(0, LEAD), :], lead.at[u + 2, pl.ds(LEAD, GROUP), :], direct.at[u])
        return [
            pltpu.make_async_remote_copy(dst, dst, g_send.at[k, 0], g_recv.at[k, u], device_id=(s, u), device_id_type=MESH)
            for k, dst in enumerate(dsts)
        ]

    @pl.loop(1, n)
    def _(d):
        for copy in g_copies(d):
            copy.start()

    lead[0] = jnp.zeros_like(lead[0])
    lead[1] = jnp.zeros_like(lead[1])
    lead[n + 2] = jnp.zeros_like(lead[n + 2])
    mine = pl.ds(pl.multiple_of(core * half, half), half)
    lead[t + 2, 0:LEAD, :] = coef[0:LEAD, mine]
    lead[t + 2, LEAD : LEAD + GROUP, :] = coef[group(s), mine]
    pair = lax.div(t, 2)
    direct[t] = coef[pl.ds(pl.multiple_of(pair * 2 * GROUP, 2 * GROUP), 2 * GROUP), mine]

    @pl.loop(1, n)
    def _(d):
        for copy in g_arrivals(lax.rem(t + n - d, n)):
            copy.wait_recv()

    for tt in range(n):
        head[tt] = lead[tt + 2, 0:LEAD, :].astype(F32)
        at = slice(tt * half, (tt + 1) * half)
        left[rows:span, at] = direct[tt, 0:GROUP, :]
        left[span + rows : 2 * span, at] = direct[tt, GROUP : 2 * GROUP, :]
        right[rows:span, at] = lead[tt + 3, LEAD : LEAD + GROUP, :]
        right[span : span + GROUP, at] = lead[tt + 2, LEAD : LEAD + GROUP, :]

    products = LEAD * jblocks

    def features(dst, base, block):
        @pl.loop(0, per_block)
        def _(k):
            q = jnp.maximum(block * per_block + k - n, 0)
            later = lax.div(q, products)
            q = q - later * products
            i, jb = lax.div(q, jblocks), lax.rem(q, jblocks)
            for tt in range(n):
                delayed = lead[tt + 1 - later, group(jb), :].astype(F32)
                row = head[tt, pl.ds(i, 1), :]
                at = pl.ds(pl.multiple_of(base + k * GROUP, GROUP), GROUP)
                dst[at, tt * half : (tt + 1) * half] = (row * delayed).astype(BF16)

    features(left, 0, 2 * pair)
    features(left, span, 2 * pair + 1)
    features(right, 0, s)

    acc[...] = jnp.zeros_like(acc)
    wide = 4 * half

    @pl.loop(0, n // 4)
    def _(c):
        at = pl.ds(pl.multiple_of(c * wide, wide), wide)
        acc[:, 0 : span + GROUP] += lax.dot_general(
            left[:, at], right[:, at], (((1,), (1,)), ((), ())), preferred_element_type=F32
        )

    swap = pltpu.make_async_remote_copy(
        acc.at[pl.ds(pl.multiple_of((1 - core) * span, GROUP), span), :], sib, sib_send, sib_recv,
        device_id=(s, other), device_id_type=MESH,
    )
    swap.start()
    fin[...] = jnp.zeros_like(fin)
    swap.wait()
    fin[0:span, :] = acc[pl.ds(pl.multiple_of(core * span, GROUP), span), :] + sib[...]

    turned[...] = fin[:, tile0 : tile0 + 128].T
    first = span - tile0
    col_msg = turned.at[pl.ds(first, GROUP), :]

    @pl.when(s != 0)
    def _():
        copy = pltpu.make_async_remote_copy(
            col_msg, colbuf.at[group(s), :], msg_send.at[0], col_recv.at[s], device_id=(0, t), device_id_type=MESH
        )
        copy.start()
        copy.wait_send()

    @pl.when(s == 0)
    def _():
        colbuf[0:GROUP, :] = turned[first : first + GROUP, :]

        @pl.loop(1, n)
        def _(k):
            pltpu.make_async_remote_copy(
                col_msg, colbuf.at[group(k), :], msg_send.at[0], col_recv.at[k], device_id=(k, t), device_id_type=MESH
            ).wait_recv()

        fin[:, 0 : n * GROUP] = colbuf[...].T[:, 0 : n * GROUP]

    row_msg = fin.at[pl.ds(rows, GROUP), :]

    @pl.when(t != 0)
    def _():
        copy = pltpu.make_async_remote_copy(
            row_msg, rowbuf.at[group(t), :], msg_send.at[1], row_recv.at[t], device_id=(s, 0), device_id_type=MESH
        )
        copy.start()
        copy.wait_send()

    @pl.when(t == 0)
    def _():
        rowbuf[0:GROUP, :] = fin[rows:span, :]

        @pl.loop(1, n)
        def _(k):
            pltpu.make_async_remote_copy(
                row_msg, rowbuf.at[group(k), :], msg_send.at[1], row_recv.at[k], device_id=(s, k), device_id_type=MESH
            ).wait_recv()

        fin[0 : n * GROUP, :] = rowbuf[0 : n * GROUP, :]

    turned[...] = fin[:, tile0 : tile0 + 128].T
    scale = 1.0 / total
    rhs_t[...] = turned[rows - tile0 : span - tile0, 0:rows] * scale
    delta = s * rows - t * rows
    on_diagonal = (
        lax.broadcasted_iota(jnp.int32, (rows, rows), 0) == lax.broadcasted_iota(jnp.int32, (rows, rows), 1) + delta
    )
    gram[...] = fin[0:rows, 0:rows] * scale + jnp.where(on_diagonal, RIDGE, 0.0)

    @pl.loop(1, n)
    def _(d):
        rs_copy(d).wait_send()
        ag_copy(d).wait_send()
        for copy in g_copies(d):
            copy.wait_send()


def per_device(snapshots, modes, *, n):
    dof, snap = snapshots.shape
    count = modes.shape[1]
    assert count == n * GROUP
    features = count + 2 * LEAD * LEAD
    rows = features // n
    span = rows + GROUP
    tall = -(-(span + GROUP) // 128) * 128
    half = snap // 2
    chunks = 10 if dof % 2560 == 0 else 2
    depth = dof // chunks
    dma, vmem = pltpu.SemaphoreType.DMA, pltpu.VMEM
    gram, rhs_t = pl.pallas_call(
        functools.partial(kernel, n, rows // GROUP, chunks),
        out_shape=(
            jax.ShapeDtypeStruct((rows, rows), F32),
            jax.ShapeDtypeStruct((GROUP, rows), F32),
        ),
        in_specs=[pl.BlockSpec(memory_space=pl.ANY)] * 2,
        out_specs=(pl.BlockSpec(memory_space=pltpu.VMEM),) * 2,
        scratch_shapes=[
            vmem((chunks, depth, snap), BF16),
            vmem((chunks, depth, count), BF16),
            vmem((count, snap), F32),
            vmem((count, snap), BF16),
            vmem((n, GROUP, snap), BF16),
            vmem((count, snap), BF16),
            vmem((n + 3, LEAD + GROUP, half), BF16),
            vmem((n, 2 * GROUP, half), BF16),
            vmem((n, LEAD, half), F32),
            vmem((2 * span, n * half), BF16),
            vmem((span + GROUP, n * half), BF16),
            vmem((2 * span, tall), F32),
            vmem((span, tall), F32),
            vmem((tall, tall), F32),
            vmem((128, tall), F32),
            vmem((max(n * GROUP, 128), tall), F32),
            vmem((n * GROUP, tall), F32),
            dma((2, chunks)),
            dma((n,)), dma((n,)), dma((n,)), dma((n,)),
            dma((3, n)), dma((3, n)),
            dma, dma, dma((2,)), dma((n,)), dma((n,)),
        ],
        compiler_params=pltpu.CompilerParams(
            collective_id=0, has_side_effects=True, vmem_limit_bytes=60 * 1024 * 1024
        ),
    )(snapshots, modes)
    return gram, rhs_t.T


def solution(mesh):
    n = mesh.shape["tm"]
    assert mesh.shape["space"] == n
    return jax.shard_map(
        functools.partial(per_device, n=n),
        mesh=mesh,
        in_specs=(P("space", "tm"), P("space", None)),
        out_specs=(P("tm", "space"), P("tm", "space")),
        check_vma=False,
    )
```

time: 220 us -> 62.9 us (0.29)
  waiting for transfers between devices: 93.4 us -> 0 us
  blocking collectives: 84.2 us -> 0 us
  Pallas kernels: 0 us -> 58.9 us
  matrix products: 16.2 us -> 0 us
  between operations: 14.1 us -> 0.64 us
  starting transfers between devices: 5.16 us -> 0 us
  other arithmetic: 4.85 us -> 0 us
  local copies, waits for them, and re-layouts: 0.75 us -> 3.17 us
    reduce_scatter x1 -> x0, waiting for transfers between devices: 90.7 us -> none  [per_device(): lax.psum_scatter(contract_rows(phi, right), 'tm', scatter_dimension=0, ti...]
    psum x1 -> x0, blocking collectives: 84.2 us -> none  [per_device(): coeffs = lax.psum(partial_sums, 'space').astype(jnp.bfloat16)]
    pallas_call x0 -> x1, Pallas kernels: none -> 58.9 us  [per_device(): pl.pallas_call(functools.partial(kernel, n, rows // GROUP, chunks), out_s...]
    dot_general x2 -> x0, matrix products: 16.2 us -> none  [the longest x1 8.94 us: contract_rows(): lax.dot_general(left, right, (((1,), (1,)), ((), ())), preferred_element_...]
    ppermute x3 -> x0, starting transfers between devices: 5.13 us -> none  [passed_along(): lax.ppermute(value, axis, [(source, source + steps) for source in range(l...]
    ppermute x3 -> x0, waiting for transfers between devices: 2.76 us -> none  [passed_along(): lax.ppermute(value, axis, [(source, source + steps) for source in range(l...]
    unnamed x1 -> x2, local copies, waits for them, and re-layouts: 0.71 us -> 3.17 us
  transfers between devices with their start and end apart: 4 -> 0, of which waited for: 3 -> 0; matrix products, arithmetic and copies ran while one was open for 1% -> 0% of each run, Pallas kernels for 0% -> 0%
where the time goes in v1:
time: 62.9 us; the launch traced here: 62.7 us
  Pallas kernels  58.9 us (94%)
  local copies, waits for them, and re-layouts  3.17 us (5%)
  between operations  0.64 us (1%)
    pallas_call x1, Pallas kernels, per_device(): pl.pallas_call(functools.partial(kernel, n, rows // GROUP, chunks), out_s...  58.9 us
    unnamed x2, local copies, waits for them, and re-layouts  3.17 us

profile of v1, /device:TPU:0, one launch (start us, length us, event | category | flops | bytes accessed | tf_op | source)
XLA Modules:
  0.0 62.7 jit_solution(17635506338667879311)
XLA Ops:
  0.6 58.9 %shard_map.41 = (f32[304,304]{1,0:T(8,128)}, f32[16,304]{1,0:T(8,128)}) custom-call(bf16[10240,512]{1,0:T(8,128)(2,1)} %snaps.1, bf16[10240,256]{1,0:T(8,128)(2,1)} %modes.1), custom_call_target="tpu_custom_call" | custom-call | tf_op jit(solution)/shard_map/pallas_call | solution.py:280
  59.5 1.8 %copy.6 = f32[304,304]{1,0:T(8,128)} copy(f32[304,304]{1,0:T(8,128)} %get-tuple-element.8) | data formatting | bytes 739328
  61.4 1.3 %copy.7 = f32[304,16]{0,1:T(8,128)} copy(f32[304,16]{0,1:T(8,128)} %bitcast.1) | data formatting | bytes 38912

commit v2 on v1

v2 whole, which is shorter than its diff:
```python
import functools

import jax
import jax.numpy as jnp
from jax import lax
from jax.experimental import pallas as pl
from jax.experimental.pallas import tpu as pltpu
from jax.sharding import PartitionSpec as P

LEAD = 48
RIDGE = 0.05
GROUP = 16
MESH = pl.DeviceIdType.MESH
F32 = jnp.float32
BF16 = jnp.bfloat16


def kernel(
    n, per_block, chunks,
    snaps, modes, gram, rhs_t,
    sbuf, mbuf, mturn, psum, part, rsbuf, coef, stage, lead, direct, head, left, right,
    acc_a, acc_b, sib_a, sib_b, fin, turned, colmsg, rowmsg, colbuf, rowbuf,
    load_sem, rs_send, rs_recv, ag_send, ag_recv, g_send, g_recv, sib_send, sib_recv, msg_send, col_recv, row_recv,
):
    s = lax.axis_index("space")
    t = lax.axis_index("tm")
    core = lax.rem(t, 2)
    other = t + 1 - 2 * core
    pair = lax.div(t, 2)
    rows = GROUP * per_block
    span = rows + GROUP
    dof, snap = snaps.shape
    half, lanes = snap // 2, snap // 4
    depth = dof // chunks
    total = n * snap
    tile0 = (rows // 128) * 128
    jblocks = LEAD // GROUP

    def group(k):
        return pl.ds(pl.multiple_of(k * GROUP, GROUP), GROUP)

    def loads(c, h):
        at = pl.ds(pl.multiple_of(c * depth, depth), depth)
        copies = [
            pltpu.make_async_copy(
                snaps.at[at, pl.ds(k * half + h * lanes, lanes)],
                sbuf.at[h, c, :, pl.ds(k * lanes, lanes)],
                load_sem.at[2 * h + k, c],
            )
            for k in range(2)
        ]
        if h == 0:
            copies.append(pltpu.make_async_copy(modes.at[at, :], mbuf.at[c], load_sem.at[4, c]))
        return copies

    for h in range(2):

        @pl.loop(0, chunks)
        def _(c):
            for copy in loads(c, h):
                copy.start()

    barrier = pltpu.get_barrier_semaphore()

    @pl.loop(1, n)
    def _(d):
        pl.semaphore_signal(barrier, inc=1, device_id=(lax.rem(s + d, n), t), device_id_type=MESH)
        pl.semaphore_signal(barrier, inc=1, device_id=(s, lax.rem(t + d, n)), device_id_type=MESH)

    def rs_copy(h, d):
        peer = lax.rem(s + d, n)
        return pltpu.make_async_remote_copy(
            part.at[h, group(peer), :], rsbuf.at[h, s], rs_send.at[h, d], rs_recv.at[h, s],
            device_id=(peer, t), device_id_type=MESH,
        )

    def rs_arrival(h, k):
        return pltpu.make_async_remote_copy(
            part.at[h, group(k), :], rsbuf.at[h, k], rs_send.at[h, 0], rs_recv.at[h, k],
            device_id=(k, t), device_id_type=MESH,
        )

    def ag_copy(h, d):
        return pltpu.make_async_remote_copy(
            coef.at[h, group(s), :], coef.at[h, group(s), :], ag_send.at[h, d], ag_recv.at[h, s],
            device_id=(lax.rem(s + d, n), t), device_id_type=MESH,
        )

    def ag_arrival(h, k):
        return pltpu.make_async_remote_copy(
            coef.at[h, group(k), :], coef.at[h, group(k), :], ag_send.at[h, 0], ag_recv.at[h, k],
            device_id=(k, t), device_id_type=MESH,
        )

    def pair_rows(which):
        return pl.ds(pl.multiple_of(which * 2 * GROUP, 2 * GROUP), 2 * GROUP)

    def core_lanes(c):
        return pl.ds(pl.multiple_of(c * lanes, lanes), lanes)

    def g_copies(h, d):
        u = lax.rem(t + d, n)
        c = lax.rem(u, 2)
        ends = (
            (stage.at[h, c], lead.at[h, t + 2]),
            (coef.at[h, pair_rows(lax.div(u, 2)), core_lanes(c)], direct.at[h, t]),
        )
        return [
            pltpu.make_async_remote_copy(
                src, dst, g_send.at[h, k, d], g_recv.at[h, k, t], device_id=(s, u), device_id_type=MESH
            )
            for k, (src, dst) in enumerate(ends)
        ]

    def g_arrivals(h, u):
        return [
            pltpu.make_async_remote_copy(
                dst, dst, g_send.at[h, k, 0], g_recv.at[h, k, u], device_id=(s, u), device_id_type=MESH
            )
            for k, dst in enumerate((lead.at[h, u + 2], direct.at[h, u]))
        ]

    def start_rs(h):
        part[h] = psum[h].astype(BF16)
        if h == 0:
            pl.semaphore_wait(barrier, 2 * (n - 1))

        @pl.loop(1, n)
        def _(d):
            rs_copy(h, d).start()

        rsbuf[h, s] = part[h, group(s), :]

    def start_ag(h):
        @pl.loop(1, n)
        def _(d):
            rs_arrival(h, lax.rem(s + n - d, n)).wait_recv()

        value = psum[h, group(s), :] - rsbuf[h, s].astype(F32)
        for k in range(n):
            value = value + rsbuf[h, k].astype(F32)
        coef[h, group(s), :] = value.astype(BF16)

        @pl.loop(1, n)
        def _(d):
            ag_copy(h, d).start()

    def start_gather(h):
        @pl.loop(1, n)
        def _(d):
            ag_arrival(h, lax.rem(s + n - d, n)).wait_recv()

        for c in range(2):
            stage[h, c, 0:LEAD, :] = coef[h, 0:LEAD, c * lanes : (c + 1) * lanes]
            stage[h, c, LEAD : LEAD + GROUP, :] = coef[h, group(s), c * lanes : (c + 1) * lanes]

        @pl.loop(1, n)
        def _(d):
            for copy in g_copies(h, d):
                copy.start()

        lead[h, t + 2] = stage[h, core]
        direct[h, t] = coef[h, pair_rows(pair), core_lanes(core)]

    products = LEAD * jblocks

    def features(h, dst, base, block):
        @pl.loop(0, per_block)
        def _(k):
            q = jnp.maximum(block * per_block + k - n, 0)
            later = lax.div(q, products)
            q = q - later * products
            i, jb = lax.div(q, jblocks), lax.rem(q, jblocks)
            at = pl.ds(pl.multiple_of(base + k * GROUP, GROUP), GROUP)
            for tt in range(n):
                delayed = lead[h, tt + 1 - later, group(jb), :].astype(F32)
                row = head[tt, pl.ds(i, 1), :]
                dst[h, at, tt * lanes : (tt + 1) * lanes] = (row * delayed).astype(BF16)

    def build(h):
        @pl.loop(1, n)
        def _(d):
            for copy in g_arrivals(h, lax.rem(t + n - d, n)):
                copy.wait_recv()

        for tt in range(n):
            head[tt] = lead[h, tt + 2, 0:LEAD, :].astype(F32)
            at = slice(tt * lanes, (tt + 1) * lanes)
            left[h, rows:span, at] = direct[h, tt, 0:GROUP, :]
            left[h, span + rows : 2 * span, at] = direct[h, tt, GROUP : 2 * GROUP, :]
            right[h, rows:span, at] = lead[h, tt + 3, LEAD : LEAD + GROUP, :]
            right[h, span : span + GROUP, at] = lead[h, tt + 2, LEAD : LEAD + GROUP, :]
        features(h, right, 0, s)
        features(h, left, 0, 2 * pair)
        features(h, left, span, 2 * pair + 1)

    def contract(a, b):
        return lax.dot_general(a, b, (((1,), (1,)), ((), ())), preferred_element_type=F32)

    for h in range(2):
        psum[h] = jnp.zeros_like(psum[h])

        @pl.loop(0, chunks)
        def _(c):
            for copy in loads(c, h):
                copy.wait()
            if h == 0:
                across = mbuf[c].T
                mturn[c] = across
            else:
                across = mturn[c]
            psum[h] += jnp.dot(across, sbuf[h, c], preferred_element_type=F32)

        start_rs(h)

    for h in range(2):
        lead[h, 0] = jnp.zeros_like(lead[h, 0])
        lead[h, 1] = jnp.zeros_like(lead[h, 1])
        lead[h, n + 2] = jnp.zeros_like(lead[h, n + 2])
    fin[...] = jnp.zeros_like(fin)
    acc_b[...] = jnp.zeros_like(acc_b)
    start_ag(0)
    start_ag(1)
    start_gather(0)
    start_gather(1)

    end = span + GROUP
    build(0)
    acc_b[:, 0 : end - tile0] = contract(left[0], right[0, tile0:end, :])
    acc_a[...] = contract(left[0], right[0, 0:tile0, :])
    build(1)
    acc_b[:, 0 : end - tile0] += contract(left[1], right[1, tile0:end, :])

    theirs = pl.ds(pl.multiple_of((1 - core) * span, GROUP), span)
    ours = pl.ds(pl.multiple_of(core * span, GROUP), span)

    def swap(k, acc, sib):
        return pltpu.make_async_remote_copy(
            acc.at[theirs, :], sib, sib_send.at[k], sib_recv.at[k], device_id=(s, other), device_id_type=MESH
        )

    swap_b, swap_a = swap(0, acc_b, sib_b), swap(1, acc_a, sib_a)
    swap_b.start()
    acc_a[theirs, :] += contract(left[1, theirs, :], right[1, 0:tile0, :])
    swap_a.start()
    swap_b.wait()
    fin[0:span, tile0 : tile0 + 128] = acc_b[ours, :] + sib_b[...]

    turned[...] = fin[:, tile0 : tile0 + 128].T
    first = span - tile0
    colmsg[...] = turned[first : first + GROUP, :].astype(BF16)

    def col_copy(k, peer):
        return pltpu.make_async_remote_copy(
            colmsg, colbuf.at[group(k), :], msg_send.at[0], col_recv.at[k], device_id=(peer, t), device_id_type=MESH
        )

    @pl.when(s != 0)
    def _():
        col_copy(s, 0).start()

    acc_a[ours, :] += contract(left[1, ours, :], right[1, 0:tile0, :])
    swap_a.wait()
    fin[0:span, 0:tile0] = acc_a[ours, :] + sib_a[...]

    @pl.when(s != 0)
    def _():
        col_copy(s, 0).wait_send()

    @pl.when(s == 0)
    def _():
        colbuf[0:GROUP, :] = colmsg[...]

        @pl.loop(1, n)
        def _(k):
            col_copy(k, k).wait_recv()

        fin[:, 0 : n * GROUP] = colbuf[...].astype(F32).T[:, 0 : n * GROUP]

    def row_copy(k, peer):
        return pltpu.make_async_remote_copy(
            rowmsg, rowbuf.at[group(k), :], msg_send.at[1], row_recv.at[k], device_id=(s, peer), device_id_type=MESH
        )

    rowmsg[...] = fin[rows:span, :].astype(BF16)

    @pl.when(t != 0)
    def _():
        row_copy(t, 0).start()

    @pl.when(t == 0)
    def _():
        rowbuf[0:GROUP, :] = rowmsg[...]

        @pl.loop(1, n)
        def _(k):
            row_copy(k, k).wait_recv()

        fin[0 : n * GROUP, :] = rowbuf[...].astype(F32)

    turned[...] = fin[:, tile0 : tile0 + 128].T
    scale = 1.0 / total
    rhs_t[...] = turned[rows - tile0 : span - tile0, 0:rows] * scale
    delta = s * rows - t * rows
    on_diagonal = (
        lax.broadcasted_iota(jnp.int32, (rows, rows), 0) == lax.broadcasted_iota(jnp.int32, (rows, rows), 1) + delta
    )
    gram[...] = fin[0:rows, 0:rows] * scale + jnp.where(on_diagonal, RIDGE, 0.0)

    @pl.when(t != 0)
    def _():
        row_copy(t, 0).wait_send()

    for h in range(2):

        @pl.loop(1, n)
        def _(d):
            rs_copy(h, d).wait_send()
            ag_copy(h, d).wait_send()
            for copy in g_copies(h, d):
                copy.wait_send()


def per_device(snapshots, modes, *, n):
    dof, snap = snapshots.shape
    count = modes.shape[1]
    assert count == n * GROUP
    features = count + 2 * LEAD * LEAD
    rows = features // n
    span = rows + GROUP
    tile0 = rows // 128 * 128
    tall = tile0 + 128
    assert span + GROUP <= tall
    half, lanes = snap // 2, snap // 4
    chunks = 10 if dof % 2560 == 0 else 2
    depth = dof // chunks
    dma, vmem = pltpu.SemaphoreType.DMA, pltpu.VMEM
    gram, rhs_t = pl.pallas_call(
        functools.partial(kernel, n, rows // GROUP, chunks),
        out_shape=(
            jax.ShapeDtypeStruct((rows, rows), F32),
            jax.ShapeDtypeStruct((GROUP, rows), F32),
        ),
        in_specs=[pl.BlockSpec(memory_space=pl.ANY)] * 2,
        out_specs=(pl.BlockSpec(memory_space=pltpu.VMEM),) * 2,
        scratch_shapes=[
            vmem((2, chunks, depth, half), BF16),
            vmem((chunks, depth, count), BF16),
            vmem((chunks, count, depth), BF16),
            vmem((2, count, half), F32),
            vmem((2, count, half), BF16),
            vmem((2, n, GROUP, half), BF16),
            vmem((2, count, half), BF16),
            vmem((2, 2, LEAD + GROUP, lanes), BF16),
            vmem((2, n + 3, LEAD + GROUP, lanes), BF16),
            vmem((2, n, 2 * GROUP, lanes), BF16),
            vmem((n, LEAD, lanes), F32),
            vmem((2, 2 * span, n * lanes), BF16),
            vmem((2, span + GROUP, n * lanes), BF16),
            vmem((2 * span, tile0), F32),
            vmem((2 * span, 128), F32),
            vmem((span, tile0), F32),
            vmem((span, 128), F32),
            vmem((tall, tall), F32),
            vmem((128, tall), F32),
            vmem((GROUP, tall), BF16),
            vmem((GROUP, tall), BF16),
            vmem((max(n * GROUP, 128), tall), BF16),
            vmem((n * GROUP, tall), BF16),
            dma((5, chunks)),
            dma((2, n)), dma((2, n)), dma((2, n)), dma((2, n)),
            dma((2, 2, n)), dma((2, 2, n)),
            dma((2,)), dma((2,)), dma((2,)), dma((n,)), dma((n,)),
        ],
        compiler_params=pltpu.CompilerParams(
            collective_id=0, has_side_effects=True, vmem_limit_bytes=51 * 1024 * 1024
        ),
    )(snapshots, modes)
    return gram, rhs_t.T


def solution(mesh):
    n = mesh.shape["tm"]
    assert mesh.shape["space"] == n
    return jax.shard_map(
        functools.partial(per_device, n=n),
        mesh=mesh,
        in_specs=(P("space", "tm"), P("space", None)),
        out_specs=(P("tm", "space"), P("tm", "space")),
        check_vma=False,
    )
```

time: 62.9 us -> 53.9 us (0.86)
  Pallas kernels: 58.9 us -> 51.8 us
  local copies, waits for them, and re-layouts: 3.17 us -> 1.38 us
    pallas_call x1, Pallas kernels: 58.9 us -> 51.8 us  [per_device(): pl.pallas_call(functools.partial(kernel, n, rows // GROUP, chunks), out_s...]
    unnamed x2, local copies, waits for them, and re-layouts: 3.17 us -> 1.38 us
where the time goes in v2:
time: 53.9 us; the launch traced here: 53.8 us
  Pallas kernels  51.8 us (96%)
  local copies, waits for them, and re-layouts  1.38 us (3%)
  between operations  0.64 us (1%)
    pallas_call x1, Pallas kernels, per_device(): pl.pallas_call(functools.partial(kernel, n, rows // GROUP, chunks), out_s...  51.8 us
    unnamed x2, local copies, waits for them, and re-layouts  1.38 us

profile of v2, /device:TPU:0, one launch (start us, length us, event | category | flops | bytes accessed | tf_op | source)
XLA Modules:
  0.0 53.8 jit_solution(12707357413841867026)
XLA Ops:
  0.6 51.8 %shard_map.41 = (f32[304,304]{1,0:T(8,128)S(1)}, f32[16,304]{1,0:T(8,128)S(1)}) custom-call(bf16[10240,512]{1,0:T(8,128)(2,1)} %snaps.1, bf16[10240,256]{1,0:T(8,128)(2,1)} %modes.1), custom_call_target="tpu_custom_call" | custom-call | tf_op jit(solution)/shard_map/pallas_call | solution.py:338
  52.5 0.8 %copy.6 = f32[304,304]{1,0:T(8,128)} copy(f32[304,304]{1,0:T(8,128)S(1)} %get-tuple-element.8) | data formatting | bytes 739328
  53.2 0.6 %copy.7 = f32[304,16]{0,1:T(8,128)} copy(f32[304,16]{0,1:T(8,128)S(1)} %bitcast.1) | data formatting | bytes 38912
